TPU v7x, 32 devices: a whole 2x2x4 slice. The times are simulated.
32 devices in a mesh: dp: 4 (over z), mp: 8 (over y, x, core).
Axes of the slice: x: 2, y: 2, z: 4, core: 2. Of those that a mesh axis runs over, the one named last changes fastest.
Arguments:
- gate_pre: bfloat16 [768, 14336], P('dp', 'mp'), may hold values from -8 to 8
- up_pre: bfloat16 [768, 14336], P('dp', 'mp'), may hold values from -6 to 6
- d_out: bfloat16 [768, 4096], P(('dp', 'mp')), may hold values from -6 to 6
- down_weight: bfloat16 [4096, 14336], P('dp', 'mp'), may hold values from -0.046875 to 0.046875
Outputs:
- d_gate: bfloat16 [768, 14336], P('dp', 'mp')
- d_up: bfloat16 [768, 14336], P('dp', 'mp')
- grad_down: bfloat16 [4096, 14336], P('dp', 'mp')
All inputs are finite; a program needn't handle non-finite values.
Results may differ from a plain program's by a relative error of at most 0.0095.
Values may be sent and summed in bfloat16 or wider, within the bound.
A program may use at most 128 MiB of HBM per device.

v0:
```python
import jax
import jax.numpy as jnp
from jax import lax
from jax.sharding import PartitionSpec as P


def body(gate_pre, up_pre, d_out, down_weight):
    gate = gate_pre.astype(jnp.float32)
    upper = up_pre.astype(jnp.float32)
    sig = jax.nn.sigmoid(gate)
    act = gate * sig
    hidden = (act * upper).astype(jnp.bfloat16)
    replicas = lax.axis_size("dp")
    full_out = lax.all_gather(d_out, "mp", axis=0, tiled=True)
    tok_rows = full_out.shape[0]
    local_hidden = hidden.shape[1]
    columns = full_out
    d_hidden = jnp.dot(
        columns,
        lax.all_gather(down_weight, "dp", axis=0, tiled=True),
        preferred_element_type=jnp.float32,
    )
    d_up = (d_hidden * act).astype(jnp.bfloat16)
    d_gate = (d_hidden * upper * sig * (1.0 + gate * (1.0 - sig))).astype(jnp.bfloat16)
    feature_rows = down_weight.shape[0]
    moved = lax.all_to_all(full_out, "dp", split_axis=1, concat_axis=0, tiled=True)
    piece = lax.all_gather(hidden, "dp", axis=0, tiled=True)
    blocks = piece.shape[0] // tok_rows
    columns = moved
    terms = jnp.einsum(
        "rtd,rtf->rdf",
        columns.reshape(blocks, tok_rows, feature_rows),
        piece.reshape(blocks, tok_rows, local_hidden),
        preferred_element_type=jnp.float32,
    )
    total = jnp.sum(terms.astype(jnp.bfloat16).astype(jnp.float32), axis=0)
    grad_down = (total / replicas).astype(jnp.bfloat16)
    return (d_gate, d_up, grad_down)


def solution(mesh):
    in_specs = (P("dp", "mp"), P("dp", "mp"), P(("dp", "mp"), None), P("dp", "mp"))
    out_specs = (P("dp", "mp"), P("dp", "mp"), P("dp", "mp"))
    return jax.shard_map(body, mesh=mesh, in_specs=in_specs, out_specs=out_specs, check_vma=False)
```

profile of v0, /device:TPU:0, one launch (start us, length us, event | category | flops | bytes accessed | tf_op | source)
XLA Modules:
  0.0 415.6 jit_solution(11324991727766426773)
XLA Ops:
  7.2 0.0 all-gather.4.cloned.1.call-start
  7.2 0.7 all-gather.4.cloned.1.call-update
  7.9 0.0 copy-start.1
  7.9 0.0 copy-start.2
  7.9 0.0 all-gather.6.cloned.1.call-start
  8.0 0.7 all-gather.6.cloned.1.call-update
  8.7 0.0 all-gather.8.cloned.1.call-start
  8.7 29.6 %all-gather.4.cloned.1.call-done = bf16[192,4096]{1,0:T(8,128)(2,1)} async-done(((bf16[24,4096]{1,0:T(8,128)(2,1)}), bf16[192,4096]{1,0:T(8,128)(2,1)}) %all-gather.4.cloned.1.call-update) | async-done | bytes 1572880 | tf_op jit(solution)/shard_map/all_gather | solution.py:14
  38.3 254.1 %all-gather.6.cloned.1.call-done = bf16[4096,1792]{1,0:T(8,128)(2,1)} async-done(((bf16[1024,1792]{1,0:T(8,128)(2,1)}), bf16[4096,1792]{1,0:T(8,128)(2,1)}) %all-gather.6.cloned.1.call-update) | async-done | bytes 14680080 | tf_op jit(solution)/shard_map/all_gather | solution.py:20
  292.4 0.0 copy-done.1
  292.4 0.0 copy-done.2
  292.4 0.0 copy-start
  292.4 10.4 %multiply_convert_fusion.1 = (bf16[192,1792]{1,0:T(8,128)(2,1)}, bf16[192,1792]{1,0:T(8,128)(2,1)}, bf16[192,1792]{1,0:T(8,128)(2,1)}) fusion(bf16[192,1792]{1,0:T(8,128)(2,1)S(1)} %copy-done.1, bf16[192,1792]{1,0:T(8,128)(2,1)S(1)} %copy-done.2, bf16[192,4096]{1,0:T(8,128)(2,1)} %all-gather.4.cloned.1.call-done, ...), kind=kOutput, calls=%fused_computation.18 | convolution fusion | flops 2824421376 | bytes 19693568 | tf_op jit(solution)/shard_map/dot_general | solution.py:18
  302.8 0.0 all-gather.8.cloned.1.call-update
  302.8 0.0 copy-done
  302.8 0.1 copy.12
  303.0 77.7 %all_to_all.16 = bf16[192,4,1024]{2,0,1:T(8,128)(2,1)S(1)} all-to-all(bf16[192,4,1024]{2,0,1:T(8,128)(2,1)S(1)} %bitcast.13), channel_id=1, replica_groups=mesh['dp'=4,'mp'=8] {'dp'}, dimensions={1} | all-to-all | bytes 3145728 | tf_op jit(solution)/shard_map/all_to_all | solution.py:26
  380.6 6.8 %all-gather.8.cloned.1.call-done = bf16[768,1792]{1,0:T(8,128)(2,1)} async-done(((bf16[192,1792]{1,0:T(8,128)(2,1)}), bf16[768,1792]{1,0:T(8,128)(2,1)}) %all-gather.8.cloned.1.call-update) | async-done | bytes 2752528 | tf_op jit(solution)/shard_map/all_gather | solution.py:27
  387.5 9.6 %convert_reduce_fusion = f32[1792,1024]{1,0:T(8,128)} fusion(bf16[4,192,1792]{2,1,0:T(8,128)(2,1)} %bitcast.15, bf16[192,4,1024]{2,0,1:T(8,128)(2,1)S(1)} %all_to_all.16), kind=kOutput, calls=%fused_computation | convolution fusion | flops 2838757376 | bytes 11665408 | tf_op jit(solution)/shard_map/rtd,rtf->rdf/dot_general | solution.py:30
  397.0 6.1 %fusion = bf16[1024,1792]{0,1:T(8,128)(2,1)} fusion(f32[1792,1024]{1,0:T(8,128)} %convert_reduce_fusion), kind=kLoop, calls=%fused_computation.2 | loop fusion | flops 3670016 | bytes 11010048 | tf_op jit(solution)/shard_map/convert_element_type | solution.py:37
  403.1 5.9 %copy.9 = bf16[1024,1792]{1,0:T(8,128)(2,1)} copy(bf16[1024,1792]{0,1:T(8,128)(2,1)} %fusion) | data formatting | bytes 7340032
Async XLA Ops:
  7.2 31.1 %all-gather.4.cloned.1.call-start = ((), (), s32[]{:S(2)}) async-start(), calls=%async_computation.1 | async-start | bytes 1769472 | tf_op jit(solution)/shard_map/all_gather | solution.py:14
  7.9 284.5 %copy-start.1 = (bf16[192,1792]{1,0:T(8,128)(2,1)S(1)}, bf16[192,1792]{1,0:T(8,128)(2,1)}, u32[]{:S(2)}) copy-start(bf16[192,1792]{1,0:T(8,128)(2,1)} %param.4) | copy-start | bytes 2064388
  7.9 284.5 %copy-start.2 = (bf16[192,1792]{1,0:T(8,128)(2,1)S(1)}, bf16[192,1792]{1,0:T(8,128)(2,1)}, u32[]{:S(2)}) copy-start(bf16[192,1792]{1,0:T(8,128)(2,1)} %param.5) | copy-start | bytes 2064388
  7.9 284.5 %all-gather.6.cloned.1.call-start = ((), (), s32[]{:S(2)}) async-start(), calls=%async_computation.2 | async-start | bytes 18350080 | tf_op jit(solution)/shard_map/all_gather | solution.py:20
  8.7 378.8 %all-gather.8.cloned.1.call-start = ((), (), s32[]{:S(2)}) async-start(), calls=%async_computation.3 | async-start | bytes 3440640 | tf_op jit(solution)/shard_map/all_gather | solution.py:27
  292.4 10.4 %copy-start = (bf16[192,4096]{1,0:T(8,128)(2,1)S(1)}, bf16[192,4096]{1,0:T(8,128)(2,1)}, u32[]{:S(2)}) copy-start(bf16[192,4096]{1,0:T(8,128)(2,1)} %all-gather.4.cloned.1.call-done) | copy-start | bytes 4718596
Sparse Core Ops, SparseCore 0:
  9.9 28.3 all-gather.3
  39.9 252.4 all-gather.5
  302.9 84.5 all-gather.7
where the time goes:
time: 416 us
  waiting for transfers between devices  292 us (70%)
  blocking collectives  77.7 us (19%)
  matrix products  19.9 us (5%)
  between operations  13.8 us (3%)
  other arithmetic  6.09 us (1%)
  local copies, waits for them, and re-layouts  6.06 us (1%)
    all_gather x1, waiting for transfers between devices, body(): lax.all_gather(down_weight, 'dp', axis=0, tiled=True)  254 us
    all_to_all x1, blocking collectives, body(): lax.all_to_all(full_out, 'dp', split_axis=1, concat_axis=0, tiled=True)  77.7 us
    all_gather x1, waiting for transfers between devices, body(): full_out = lax.all_gather(d_out, 'mp', axis=0, tiled=True)  29.6 us
    dot_general x1, matrix products, body(): jnp.dot(columns, lax.all_gather(down_weight, 'dp', axis=0, tiled=True), p...  10.4 us
    dot_general x1, matrix products, body(): jnp.einsum('rtd,rtf->rdf', columns.reshape(blocks, tok_rows, feature_rows...  9.56 us
  transfers between devices with their start and end apart: 3, of which 3 were waited for; matrix products, arithmetic and copies ran while one was open for 0% of the time, Pallas kernels for 0%

commit v1 on v0

--- a/solution.py
+++ b/solution.py
@@ -2,16 +2,32 @@
 import jax.numpy as jnp
 from jax import lax
 from jax.sharding import PartitionSpec as P
+from jax.lax import axis_index, ppermute, psum
 
 
 def body(gate_pre, up_pre, d_out, down_weight):
+
+    def write_the_tables(chip_axis, array_dim, m):
+        nodes = psum(1, axis_name=chip_axis)
+        clean = map(lambda k: (k - 1, k), range(1, nodes))
+        q_next = list(clean)
+        w1 = q_next + [(nodes - 1, 0)]
+        y_new = m
+        heap = [y_new]
+        for _ in range(nodes - 1):
+            y_new = ppermute(y_new, axis_name=chip_axis, perm=w1)
+            heap += [y_new]
+        r2 = jnp.concatenate([*reversed(heap)], array_dim)
+        a_now = jnp.roll(r2, (axis_index(chip_axis) + 1) * y_new.shape[array_dim], array_dim)
+        return a_now
+
     gate = gate_pre.astype(jnp.float32)
     upper = up_pre.astype(jnp.float32)
     sig = jax.nn.sigmoid(gate)
     act = gate * sig
     hidden = (act * upper).astype(jnp.bfloat16)
     replicas = lax.axis_size("dp")
-    full_out = lax.all_gather(d_out, "mp", axis=0, tiled=True)
+    full_out = write_the_tables("mp", 0, d_out)
     tok_rows = full_out.shape[0]
     local_hidden = hidden.shape[1]
     columns = full_out

time: 416 us -> 381 us (0.916)
  waiting for transfers between devices: 292 us -> 263 us
  local copies, waits for them, and re-layouts: 6.06 us -> 0.92 us
    ppermute x0 -> x7, waiting for transfers between devices: none -> 42.2 us  [write_the_tables(): y_new = ppermute(y_new, axis_name=chip_axis, perm=w1)]
    all_gather x1, waiting for transfers between devices: 254 us -> 213 us  [body(): lax.all_gather(down_weight, 'dp', axis=0, tiled=True)]
    all_gather x1 -> x0, waiting for transfers between devices: 29.6 us -> none  [body(): full_out = lax.all_gather(d_out, 'mp', axis=0, tiled=True)]
    unnamed x7 -> x21, local copies, waits for them, and re-layouts: 5.92 us -> 0.38 us
  transfers between devices with their start and end apart: 3 -> 9, of which waited for: 3 -> 9; matrix products, arithmetic and copies ran while one was open for 0% -> 0% of each run, Pallas kernels for 0% -> 0%
where the time goes in v1:
time: 381 us
  waiting for transfers between devices  263 us (69%)
  blocking collectives  77.7 us (20%)
  matrix products  19.3 us (5%)
  between operations  14.2 us (4%)
  other arithmetic  5.48 us (1%)
    all_gather x1, waiting for transfers between devices, body(): lax.all_gather(down_weight, 'dp', axis=0, tiled=True)  213 us
    all_to_all x1, blocking collectives, body(): lax.all_to_all(full_out, 'dp', split_axis=1, concat_axis=0, tiled=True)  77.7 us
    ppermute x7, waiting for transfers between devices, write_the_tables(): y_new = ppermute(y_new, axis_name=chip_axis, perm=w1)  42.2 us
    dot_general x1, matrix products, body(): jnp.dot(columns, lax.all_gather(down_weight, 'dp', axis=0, tiled=True), p...  9.78 us
    dot_general x1, matrix products, body(): jnp.einsum('rtd,rtf->rdf', columns.reshape(blocks, tok_rows, feature_rows...  9.5 us
  transfers between devices with their start and end apart: 9, of which 9 were waited for; matrix products, arithmetic and copies ran while one was open for 0% of the time, Pallas kernels for 0%

profile of v1, /device:TPU:0, one launch (start us, length us, event | category | flops | bytes accessed | tf_op | source)
XLA Modules:
  0.0 381.1 jit_solution(1216410124087300782)
XLA Ops:
  7.2 0.0 copy-start
  7.2 0.0 all-gather.3.cloned.1.call-start
  7.2 0.7 all-gather.3.cloned.1.call-update
  7.9 0.0 all-gather.5.cloned.1.call-start
  8.0 0.1 copy-done
  8.1 0.5 collective-permute-start
  8.5 6.2 %collective-permute-done = bf16[24,4096]{1,0:T(8,128)(2,1)S(1)} collective-permute-done((bf16[24,4096]{1,0:T(8,128)(2,1)S(1)}, bf16[24,4096]{1,0:T(8,128)(2,1)S(1)}, u32[]{:S(2)}, u32[]{:S(2)}) %collective-permute-start) | collective-permute-done | bytes 196640 | tf_op jit(solution)/shard_map/ppermute | solution.py:18
  14.8 0.0 collective-permute-start.1
  14.8 6.0 %collective-permute-done.1 = bf16[24,4096]{1,0:T(8,128)(2,1)S(1)} collective-permute-done((bf16[24,4096]{1,0:T(8,128)(2,1)S(1)}, bf16[24,4096]{1,0:T(8,128)(2,1)S(1)}, u32[]{:S(2)}, u32[]{:S(2)}) %collective-permute-start.1) | collective-permute-done | bytes 196640 | tf_op jit(solution)/shard_map/ppermute | solution.py:18
  20.8 0.0 collective-permute-start.2
  20.8 6.0 %collective-permute-done.2 = bf16[24,4096]{1,0:T(8,128)(2,1)S(1)} collective-permute-done((bf16[24,4096]{1,0:T(8,128)(2,1)S(1)}, bf16[24,4096]{1,0:T(8,128)(2,1)S(1)}, u32[]{:S(2)}, u32[]{:S(2)}) %collective-permute-start.2) | collective-permute-done | bytes 196640 | tf_op jit(solution)/shard_map/ppermute | solution.py:18
  26.8 0.0 collective-permute-start.3
  26.8 6.0 %collective-permute-done.3 = bf16[24,4096]{1,0:T(8,128)(2,1)S(1)} collective-permute-done((bf16[24,4096]{1,0:T(8,128)(2,1)S(1)}, bf16[24,4096]{1,0:T(8,128)(2,1)S(1)}, u32[]{:S(2)}, u32[]{:S(2)}) %collective-permute-start.3) | collective-permute-done | bytes 196640 | tf_op jit(solution)/shard_map/ppermute | solution.py:18
  32.8 0.0 collective-permute-start.4
  32.8 6.0 %collective-permute-done.4 = bf16[24,4096]{1,0:T(8,128)(2,1)S(1)} collective-permute-done((bf16[24,4096]{1,0:T(8,128)(2,1)S(1)}, bf16[24,4096]{1,0:T(8,128)(2,1)S(1)}, u32[]{:S(2)}, u32[]{:S(2)}) %collective-permute-start.4) | collective-permute-done | bytes 196640 | tf_op jit(solution)/shard_map/ppermute | solution.py:18
  38.8 0.0 collective-permute-start.5
  38.8 6.0 %collective-permute-done.5 = bf16[24,4096]{1,0:T(8,128)(2,1)S(1)} collective-permute-done((bf16[24,4096]{1,0:T(8,128)(2,1)S(1)}, bf16[24,4096]{1,0:T(8,128)(2,1)S(1)}, u32[]{:S(2)}, u32[]{:S(2)}) %collective-permute-start.5) | collective-permute-done | bytes 196640 | tf_op jit(solution)/shard_map/ppermute | solution.py:18
  44.8 0.0 collective-permute-start.6
  44.8 6.0 %collective-permute-done.6 = bf16[24,4096]{1,0:T(8,128)(2,1)S(1)} collective-permute-done((bf16[24,4096]{1,0:T(8,128)(2,1)S(1)}, bf16[24,4096]{1,0:T(8,128)(2,1)S(1)}, u32[]{:S(2)}, u32[]{:S(2)}) %collective-permute-start.6) | collective-permute-done | bytes 196640 | tf_op jit(solution)/shard_map/ppermute | solution.py:18
  50.9 0.0 copy-start.1
  50.9 0.0 copy-start.2
  51.1 0.4 constant_dynamic-slice_fusion
  51.5 213.3 %all-gather.3.cloned.1.call-done = bf16[4096,1792]{1,0:T(8,128)(2,1)} async-done(((bf16[1024,1792]{1,0:T(8,128)(2,1)}), bf16[4096,1792]{1,0:T(8,128)(2,1)}) %all-gather.3.cloned.1.call-update) | async-done | bytes 14680080 | tf_op jit(solution)/shard_map/all_gather | solution.py:36
  264.8 0.0 copy-done.1
  264.8 0.0 copy-done.2
  264.8 9.8 %multiply_convert_fusion.1 = (bf16[192,1792]{1,0:T(8,128)(2,1)}, bf16[192,1792]{1,0:T(8,128)(2,1)}, bf16[192,1792]{1,0:T(8,128)(2,1)}) fusion(bf16[192,1792]{1,0:T(8,128)(2,1)S(1)} %copy-done.1, bf16[192,1792]{1,0:T(8,128)(2,1)S(1)} %copy-done.2, bf16[192,4096]{1,0:T(8,128)(2,1)S(1)} %constant_dynamic-slice_fusion, ...), kind=kOutput, calls=%fused_computation.17 | convolution fusion | flops 2824421376 | bytes 19693568 | tf_op jit(solution)/shard_map/dot_general | solution.py:34
  274.6 0.0 all-gather.5.cloned.1.call-update
  274.6 0.1 copy.10
  274.8 77.7 %all_to_all.16 = bf16[192,4,1024]{2,0,1:T(8,128)(2,1)S(1)} all-to-all(bf16[192,4,1024]{2,0,1:T(8,128)(2,1)S(1)} %bitcast.11), channel_id=1, replica_groups=mesh['dp'=4,'mp'=8] {'dp'}, dimensions={1} | all-to-all | bytes 3145728 | tf_op jit(solution)/shard_map/all_to_all | solution.py:42
  352.4 6.8 %all-gather.5.cloned.1.call-done = bf16[768,1792]{1,0:T(8,128)(2,1)} async-done(((bf16[192,1792]{1,0:T(8,128)(2,1)}), bf16[768,1792]{1,0:T(8,128)(2,1)}) %all-gather.5.cloned.1.call-update) | async-done | bytes 2752528 | tf_op jit(solution)/shard_map/all_gather | solution.py:43
  359.3 9.5 %convert_reduce_fusion = f32[1024,1792]{1,0:T(8,128)} fusion(bf16[4,192,1792]{2,1,0:T(8,128)(2,1)} %bitcast.13, bf16[192,4,1024]{2,0,1:T(8,128)(2,1)S(1)} %all_to_all.16), kind=kOutput, calls=%fused_computation | convolution fusion | flops 2838757376 | bytes 11665408 | tf_op jit(solution)/shard_map/rtd,rtf->rdf/dot_general | solution.py:46
  368.8 5.5 %multiply_convert_fusion = bf16[1024,1792]{1,0:T(8,128)(2,1)} fusion(f32[1024,1792]{1,0:T(8,128)} %convert_reduce_fusion), kind=kLoop, calls=%fused_computation.1 | loop fusion | flops 3670016 | bytes 11010048 | tf_op jit(solution)/shard_map/convert_element_type | solution.py:53
  (16 shorter events, 0.2 us)
Async XLA Ops:
  7.2 0.9 copy-start
  7.2 257.6 %all-gather.3.cloned.1.call-start = ((), (), s32[]{:S(2)}) async-start(), calls=%async_computation.1 | async-start | bytes 18350080 | tf_op jit(solution)/shard_map/all_gather | solution.py:36
  7.9 351.4 %all-gather.5.cloned.1.call-start = ((), (), s32[]{:S(2)}) async-start(), calls=%async_computation.2 | async-start | bytes 3440640 | tf_op jit(solution)/shard_map/all_gather | solution.py:43
  8.1 6.7 %collective-permute-start = (bf16[24,4096]{1,0:T(8,128)(2,1)S(1)}, bf16[24,4096]{1,0:T(8,128)(2,1)S(1)}, u32[]{:S(2)}, u32[]{:S(2)}) collective-permute-start(bf16[24,4096]{1,0:T(8,128)(2,1)S(1)} %copy-done), channel_id=1, source_target_pairs={{0,1},{1,2},{2,3},{3,4},{4,5},{5,6},{6,7},{7,0},{8,9},{9,10},{10,1... | collective-permute-start | bytes 589832 | tf_op jit(solution)/shard_map/ppermute | solution.py:18
  14.8 6.0 %collective-permute-start.1 = (bf16[24,4096]{1,0:T(8,128)(2,1)S(1)}, bf16[24,4096]{1,0:T(8,128)(2,1)S(1)}, u32[]{:S(2)}, u32[]{:S(2)}) collective-permute-start(bf16[24,4096]{1,0:T(8,128)(2,1)S(1)} %collective-permute-done), channel_id=1, source_target_pairs={{0,1},{1,2},{2,3},{3,4},{4,5},{5,6},{6,7},{7,0},{8,9},{9,10},{10,1... | collective-permute-start | bytes 589832 | tf_op jit(solution)/shard_map/ppermute | solution.py:18
  20.8 6.0 %collective-permute-start.2 = (bf16[24,4096]{1,0:T(8,128)(2,1)S(1)}, bf16[24,4096]{1,0:T(8,128)(2,1)S(1)}, u32[]{:S(2)}, u32[]{:S(2)}) collective-permute-start(bf16[24,4096]{1,0:T(8,128)(2,1)S(1)} %collective-permute-done.1), channel_id=1, source_target_pairs={{0,1},{1,2},{2,3},{3,4},{4,5},{5,6},{6,7},{7,0},{8,9},{9,10},{10,1... | collective-permute-start | bytes 589832 | tf_op jit(solution)/shard_map/ppermute | solution.py:18
  26.8 6.0 %collective-permute-start.3 = (bf16[24,4096]{1,0:T(8,128)(2,1)S(1)}, bf16[24,4096]{1,0:T(8,128)(2,1)S(1)}, u32[]{:S(2)}, u32[]{:S(2)}) collective-permute-start(bf16[24,4096]{1,0:T(8,128)(2,1)S(1)} %collective-permute-done.2), channel_id=1, source_target_pairs={{0,1},{1,2},{2,3},{3,4},{4,5},{5,6},{6,7},{7,0},{8,9},{9,10},{10,1... | collective-permute-start | bytes 589832 | tf_op jit(solution)/shard_map/ppermute | solution.py:18
  32.8 6.0 %collective-permute-start.4 = (bf16[24,4096]{1,0:T(8,128)(2,1)S(1)}, bf16[24,4096]{1,0:T(8,128)(2,1)S(1)}, u32[]{:S(2)}, u32[]{:S(2)}) collective-permute-start(bf16[24,4096]{1,0:T(8,128)(2,1)S(1)} %collective-permute-done.3), channel_id=1, source_target_pairs={{0,1},{1,2},{2,3},{3,4},{4,5},{5,6},{6,7},{7,0},{8,9},{9,10},{10,1... | collective-permute-start | bytes 589832 | tf_op jit(solution)/shard_map/ppermute | solution.py:18
  38.8 6.0 %collective-permute-start.5 = (bf16[24,4096]{1,0:T(8,128)(2,1)S(1)}, bf16[24,4096]{1,0:T(8,128)(2,1)S(1)}, u32[]{:S(2)}, u32[]{:S(2)}) collective-permute-start(bf16[24,4096]{1,0:T(8,128)(2,1)S(1)} %collective-permute-done.4), channel_id=1, source_target_pairs={{0,1},{1,2},{2,3},{3,4},{4,5},{5,6},{6,7},{7,0},{8,9},{9,10},{10,1... | collective-permute-start | bytes 589832 | tf_op jit(solution)/shard_map/ppermute | solution.py:18
  44.8 6.0 %collective-permute-start.6 = (bf16[24,4096]{1,0:T(8,128)(2,1)S(1)}, bf16[24,4096]{1,0:T(8,128)(2,1)S(1)}, u32[]{:S(2)}, u32[]{:S(2)}) collective-permute-start(bf16[24,4096]{1,0:T(8,128)(2,1)S(1)} %collective-permute-done.5), channel_id=1, source_target_pairs={{0,1},{1,2},{2,3},{3,4},{4,5},{5,6},{6,7},{7,0},{8,9},{9,10},{10,1... | collective-permute-start | bytes 589832 | tf_op jit(solution)/shard_map/ppermute | solution.py:18
  50.9 213.9 %copy-start.1 = (bf16[192,1792]{1,0:T(8,128)(2,1)S(1)}, bf16[192,1792]{1,0:T(8,128)(2,1)}, u32[]{:S(2)}) copy-start(bf16[192,1792]{1,0:T(8,128)(2,1)} %param.4) | copy-start | bytes 2064388
  50.9 213.9 %copy-start.2 = (bf16[192,1792]{1,0:T(8,128)(2,1)S(1)}, bf16[192,1792]{1,0:T(8,128)(2,1)}, u32[]{:S(2)}) copy-start(bf16[192,1792]{1,0:T(8,128)(2,1)} %param.5) | copy-start | bytes 2064388
Sparse Core Ops, SparseCore 0:
  9.6 255.1 all-gather.2
  274.7 84.4 all-gather.4
